TPU v7x, 512 devices: a whole 4x4x16 slice. The times are simulated.
512 devices in a mesh: occ: 16 (over x_hi, y, core), vir: 32 (over z, x_lo).
Axes of the slice: x: 4 (x_hi: 2, x_lo: 2; x = x_hi * 2 + x_lo), y: 4, z: 16, core: 2. Of those that a mesh axis runs over, the one named last changes fastest.
Arguments:
- orbitals: bfloat16 [16, 8192, 4096], P('occ', 'vir'), may hold values from -0.75 to 0.75
- eps_occ: bfloat16 [16], P('occ'), may hold values from -2.5 to -0.5
- eps_vir: bfloat16 [8192], P('vir'), may hold values from 0.5 to 3
Outputs:
- density: bfloat16 [16, 8192, 4096], P('occ', 'vir')
All inputs are finite; a program needn't handle non-finite values.
Results may differ from a plain program's by a relative error of at most 0.0047.
Values may be sent and summed in bfloat16 or wider, within the bound.
No kernel may reach another device: no remote copies, remote signals or barrier semaphores. Data moves between devices by JAX's collectives and lax.ppermute only.
A program may use at most 64 MiB of HBM per device.

v0:
```python
import jax
import jax.numpy as jnp
from jax import lax
from jax.sharding import PartitionSpec as P

BATCH_DEV = 8
REACH = 1


def shifted_2(block, axis, distance):
    devices = range(lax.axis_size(axis))
    route = [((i - distance) % len(devices), i) for i in devices]
    return lax.ppermute(block, axis, route)


def pair_energies(eps_occ, occ_stack, eps_vir, batch_energy):
    own_energy = eps_occ.astype(jnp.float32)
    others = occ_stack.astype(jnp.float32)
    vir_energy = eps_vir.astype(jnp.float32)
    batch_virt = batch_energy.astype(jnp.float32)
    return (
        vir_energy[None, :, None, None, None]
        + batch_virt[None, None, None, None, :]
        - own_energy[:, None, None, None, None]
        - others[None, None, :, :, None]
    )


def shards(orbitals, eps_occ, eps_vir):
    occ_dev, vir_dev, aux_width = orbitals.shape
    block_count = 2 * REACH + 1
    offsets = list(range(-REACH, REACH + 1))
    resident = orbitals.reshape(occ_dev * vir_dev, aux_width)
    energies = []
    slices = []
    for offset in offsets:
        if offset == 0:
            slices.append(orbitals)
            energies.append(eps_occ)
        else:
            shifted, shifted_energy = shifted_2((orbitals, eps_occ), "occ", -offset)
            slices.append(shifted)
            energies.append(shifted_energy)
    stacked = jnp.stack([one_slice[:, :BATCH_DEV, :] for one_slice in slices])
    row_sets, batch_energy = (
        lax.all_gather(stacked, "vir", axis=2, tiled=True),
        lax.all_gather(eps_vir[:BATCH_DEV], "vir", axis=0, tiled=True),
    )
    batch_width = row_sets.shape[2]
    coulomb = jnp.einsum(
        "rp,cp->rc",
        resident,
        row_sets.reshape(block_count * occ_dev * batch_width, aux_width),
        preferred_element_type=jnp.float32,
    )
    coulomb = coulomb.reshape(occ_dev, vir_dev, block_count, occ_dev, batch_width)
    exchange = jnp.einsum(
        "kjap,ibp->iakjb", jnp.stack(slices), row_sets[REACH], preferred_element_type=jnp.float32
    )
    denominator = pair_energies(eps_occ, jnp.stack(energies), eps_vir, batch_energy)
    amplitude = ((2.0 * coulomb - exchange) / denominator).astype(jnp.bfloat16)
    density = jnp.dot(
        amplitude.reshape(occ_dev * vir_dev, block_count * occ_dev * batch_width),
        row_sets.reshape(block_count * occ_dev * batch_width, aux_width),
        preferred_element_type=jnp.float32,
    )
    return density.reshape(occ_dev, vir_dev, aux_width).astype(jnp.bfloat16)


def solution(mesh):
    return jax.shard_map(
        shards,
        mesh=mesh,
        in_specs=(P("occ", "vir", None), P("occ"), P("vir")),
        out_specs=P("occ", "vir", None),
        check_vma=False,
    )
```

profile of v0, /device:TPU:8, one launch (start us, length us, event | category | flops | bytes accessed | tf_op | source)
XLA Modules:
  0.0 225.0 jit_solution(18331232845301097830)
XLA Ops:
  6.5 0.0 all-gather.2.cloned.1.call-start
  6.5 1.9 collective-permute-start.1
  8.5 2.4 %collective-permute-start = (bf16[1,256,4096]{2,1,0:T(8,128)(2,1)}, bf16[1,256,4096]{2,1,0:T(8,128)(2,1)S(1)}, u32[]{:S(2)}, u32[]{:S(2)}) collective-permute-start(bf16[1,256,4096]{2,1,0:T(8,128)(2,1)} %param.3), channel_id=1, source_target_pairs={{480,0},{0,32},{32,64},{64,96},{96,128},{128,160},{160,192},{192,2... | collective-permute-start | bytes 6291464 | tf_op jit(solution)/shard_map/ppermute | solution.py:13
  10.9 0.8 slice_bitcast_fusion.12
  11.7 20.6 %collective-permute-done.1 = bf16[1,256,4096]{2,1,0:T(8,128)(2,1)S(1)} collective-permute-done((bf16[1,256,4096]{2,1,0:T(8,128)(2,1)}, bf16[1,256,4096]{2,1,0:T(8,128)(2,1)S(1)}, u32[]{:S(2)}, u32[]{:S(2)}) %collective-permute-start.1) | collective-permute-done | bytes 2097184 | tf_op jit(solution)/shard_map/ppermute | solution.py:13
  32.3 7.9 %collective-permute-done = bf16[1,256,4096]{2,1,0:T(8,128)(2,1)S(1)} collective-permute-done((bf16[1,256,4096]{2,1,0:T(8,128)(2,1)}, bf16[1,256,4096]{2,1,0:T(8,128)(2,1)S(1)}, u32[]{:S(2)}, u32[]{:S(2)}) %collective-permute-start) | collective-permute-done | bytes 2097184 | tf_op jit(solution)/shard_map/ppermute | solution.py:13
  40.2 0.0 copy-start.2
  40.2 1.3 copy-done.2
  41.5 0.7 pad_maximum_fusion
  42.2 0.0 all-gather.2.cloned.1.call-update
  42.2 1.9 collective-permute-start.2
  44.2 3.6 %collective-permute-start.3 = (bf16[1]{0:T(256)(128)(2,1)}, bf16[1]{0:T(256)(128)(2,1)}, u32[]{:S(2)}, u32[]{:S(2)}) collective-permute-start(bf16[1]{0:T(256)(128)(2,1)} %param.4), channel_id=1, source_target_pairs={{32,0},{64,32},{96,64},{128,96},{160,128},{192,160},{224,192},{256... | collective-permute-start | bytes 14 | tf_op jit(solution)/shard_map/ppermute | solution.py:13
  48.5 0.7 convert_element_type.25
  49.2 1.3 dynamic-slice
  51.2 0.9 dynamic-update-slice
  52.1 67.1 %all-reduce = bf16[256]{0:T(256)(128)(2,1)S(1)} all-reduce(bf16[256]{0:T(256)(128)(2,1)S(1)} %dynamic-update-slice), channel_id=1, replica_groups=mesh['occ'=16,'vir'=32] {'vir'}, use_global_device_ids=true, to_apply=%add | all-reduce | flops 256 | bytes 1024
  119.1 0.1 add_subtract_fusion
  119.3 0.0 collective-permute-done.2
  119.3 0.0 collective-permute-done.3
  119.3 1.4 maximum_convert_fusion
  120.7 86.0 %all-gather.2.cloned.1.call-done = bf16[3,1,256,4096]{3,2,1,0:T(8,128)(2,1)} async-done(((bf16[3,1,8,4096]{3,2,1,0:T(8,128)(2,1)}), bf16[3,1,256,4096]{3,2,1,0:T(8,128)(2,1)}) %all-gather.2.cloned.1.call-update) | async-done | bytes 6291472 | tf_op jit(solution)/shard_map/all_gather | solution.py:46
  206.6 0.0 copy-start
  206.7 0.0 copy-start.1
  206.7 0.0 copy-start.3
  206.7 5.4 %fusion.9 = f32[768,256]{1,0:T(8,128)S(1)} fusion(bf16[768,4096]{1,0:T(8,128)(2,1)} %bitcast.65, bf16[1,256,4096]{2,1,0:T(8,128)(2,1)} %param.3), kind=kOutput, calls=%fused_computation.12 | convolution fusion | flops 1610809344 | bytes 9175040 | tf_op jit(solution)/shard_map/rp,cp->rc/dot_general | solution.py:50
  212.0 0.0 copy-done
  212.1 0.4 copy-done.1
  212.5 0.6 copy-done.3
  213.1 1.9 fusion.14
  214.9 3.2 %fusion.5 = bf16[1,256,4096]{2,1,0:T(8,128)(2,1)} fusion(bf16[256,768]{0,1:T(8,128)(2,1)S(1)} %bitcast.67, bf16[768,4096]{1,0:T(8,128)(2,1)S(1)} %bitcast.66), kind=kOutput, calls=%fused_computation.7 | convolution fusion | flops 1611661312 | bytes 8781824 | tf_op jit(solution)/shard_map/dot_general | solution.py:62
  (4 shorter events, 0.0 us)
Async XLA Ops:
  6.5 200.1 %all-gather.2.cloned.1.call-start = ((), (), s32[]{:S(2)}) async-start(), calls=%async_computation | async-start | bytes 6488064 | tf_op jit(solution)/shard_map/all_gather | solution.py:46
  6.5 25.8 %collective-permute-start.1 = (bf16[1,256,4096]{2,1,0:T(8,128)(2,1)}, bf16[1,256,4096]{2,1,0:T(8,128)(2,1)S(1)}, u32[]{:S(2)}, u32[]{:S(2)}) collective-permute-start(bf16[1,256,4096]{2,1,0:T(8,128)(2,1)} %param.3), channel_id=1, source_target_pairs={{32,0},{64,32},{96,64},{128,96},{160,128},{192,160},{224,192},{256... | collective-permute-start | bytes 6291464 | tf_op jit(solution)/shard_map/ppermute | solution.py:13
  8.5 31.7 %collective-permute-start = (bf16[1,256,4096]{2,1,0:T(8,128)(2,1)}, bf16[1,256,4096]{2,1,0:T(8,128)(2,1)S(1)}, u32[]{:S(2)}, u32[]{:S(2)}) collective-permute-start(bf16[1,256,4096]{2,1,0:T(8,128)(2,1)} %param.3), channel_id=1, source_target_pairs={{480,0},{0,32},{32,64},{64,96},{96,128},{128,160},{160,192},{192,2... | collective-permute-start | bytes 6291464 | tf_op jit(solution)/shard_map/ppermute | solution.py:13
  40.2 1.3 copy-start.2
  42.2 77.0 %collective-permute-start.2 = (bf16[1]{0:T(256)(128)(2,1)}, bf16[1]{0:T(256)(128)(2,1)}, u32[]{:S(2)}, u32[]{:S(2)}) collective-permute-start(bf16[1]{0:T(256)(128)(2,1)} %param.4), channel_id=1, source_target_pairs={{480,0},{0,32},{32,64},{64,96},{96,128},{128,160},{160,192},{192,2... | collective-permute-start | bytes 14 | tf_op jit(solution)/shard_map/ppermute | solution.py:13
  44.2 75.1 %collective-permute-start.3 = (bf16[1]{0:T(256)(128)(2,1)}, bf16[1]{0:T(256)(128)(2,1)}, u32[]{:S(2)}, u32[]{:S(2)}) collective-permute-start(bf16[1]{0:T(256)(128)(2,1)} %param.4), channel_id=1, source_target_pairs={{32,0},{64,32},{96,64},{128,96},{160,128},{192,160},{224,192},{256... | collective-permute-start | bytes 14 | tf_op jit(solution)/shard_map/ppermute | solution.py:13
  206.6 5.4 %copy-start = (bf16[3,1,256,4096]{3,2,1,0:T(8,128)(2,1)S(1)}, bf16[3,1,256,4096]{3,2,1,0:T(8,128)(2,1)}, u32[]{:S(2)}) copy-start(bf16[3,1,256,4096]{3,2,1,0:T(8,128)(2,1)} %all-gather.2.cloned.1.call-done) | copy-start | bytes 18874372
  206.7 5.8 %copy-start.1 = (bf16[1,256,4096]{2,1,0:T(8,128)(2,1)S(1)}, bf16[1,256,4096]{2,1,0:T(8,128)(2,1)}, u32[]{:S(2)}) copy-start(bf16[1,256,4096]{2,1,0:T(8,128)(2,1)} %param.3) | copy-start | bytes 6291460
  206.7 6.4 %copy-start.3 = (bf16[1,256,4096]{2,1,0:T(8,128)(2,1)S(1)}, bf16[1,256,4096]{2,1,0:T(8,128)(2,1)}, u32[]{:S(2)}) copy-start(bf16[1,256,4096]{2,1,0:T(8,128)(2,1)} %copy-done.2) | copy-start | bytes 6291460
Sparse Core Ops, SparseCore 0:
  42.4 164.2 all-gather.1
where the time goes:
time: 225 us
  waiting for transfers between devices  114 us (51%)
  blocking collectives  67.1 us (30%)
  between operations  14.9 us (7%)
  matrix products  10.5 us (5%)
  starting transfers between devices  9.89 us (4%)
  local copies, waits for them, and re-layouts  5.4 us (2%)
  other arithmetic  2.84 us (1%)
    all_gather x1, waiting for transfers between devices, shards(): lax.all_gather(stacked, 'vir', axis=2, tiled=True)  86 us
    unnamed x1, blocking collectives  67.1 us
    ppermute x4, waiting for transfers between devices, shifted_2(): return lax.ppermute(block, axis, route)  28.5 us
    ppermute x4, starting transfers between devices, shifted_2(): return lax.ppermute(block, axis, route)  9.89 us
    dot_general x1, matrix products, shards(): jnp.einsum('rp,cp->rc', resident, row_sets.reshape(block_count * occ_dev...  5.38 us
    unnamed x11, local copies, waits for them, and re-layouts  4.54 us
  transfers between devices with their start and end apart: 5, of which 3 were waited for; matrix products, arithmetic and copies ran while one was open for 2% of the time, Pallas kernels for 0%

commit v1 on v0

--- a/solution.py
+++ b/solution.py
@@ -2,6 +2,7 @@
 import jax.numpy as jnp
 from jax import lax
 from jax.sharding import PartitionSpec as P
+from jax.lax import all_to_all, axis_size
 
 BATCH_DEV = 8
 REACH = 1
@@ -43,7 +44,15 @@
             energies.append(shifted_energy)
     stacked = jnp.stack([one_slice[:, :BATCH_DEV, :] for one_slice in slices])
     row_sets, batch_energy = (
-        lax.all_gather(stacked, "vir", axis=2, tiled=True),
+        jnp.concatenate(
+            all_to_all(
+                jnp.stack(axis_size("vir") * [stacked]),
+                axis_name="vir",
+                split_axis=0,
+                concat_axis=0,
+            ),
+            axis=2,
+        ),
         lax.all_gather(eps_vir[:BATCH_DEV], "vir", axis=0, tiled=True),
     )
     batch_width = row_sets.shape[2]

time: 225 us -> 389 us (1.73)
  blocking collectives: 67.1 us -> 316 us
  waiting for transfers between devices: 114 us -> 27.2 us
  between operations: 14.9 us -> 1.53 us
  starting transfers between devices: 9.89 us -> 22.4 us
  local copies, waits for them, and re-layouts: 5.4 us -> 12.3 us
    unnamed x1, blocking collectives: 67.1 us -> 316 us
    all_gather x1 -> x0, waiting for transfers between devices: 86 us -> none  [shards(): lax.all_gather(stacked, 'vir', axis=2, tiled=True)]
    all_to_all x0 -> x1, starting transfers between devices: none -> 12.5 us  [shards(): all_to_all(jnp.stack(axis_size('vir') * [stacked]), axis_name='vir', spli...]
  transfers between devices with their start and end apart: 5 -> 5, of which waited for: 3 -> 2; matrix products, arithmetic and copies ran while one was open for 2% -> 1% of each run, Pallas kernels for 0% -> 0%
where the time goes in v1:
time: 389 us; the launch traced here: 388 us
  blocking collectives  316 us (81%)
  waiting for transfers between devices  27.2 us (7%)
  starting transfers between devices  22.4 us (6%)
  local copies, waits for them, and re-layouts  12.3 us (3%)
  matrix products  6.9 us (2%)
    unnamed x1, blocking collectives  316 us
    ppermute x4, waiting for transfers between devices, shifted_2(): return lax.ppermute(block, axis, route)  27.2 us
    all_to_all x1, starting transfers between devices, shards(): all_to_all(jnp.stack(axis_size('vir') * [stacked]), axis_name='vir', spli...  12.5 us
    ppermute x4, starting transfers between devices, shifted_2(): return lax.ppermute(block, axis, route)  9.89 us
  transfers between devices with their start and end apart: 5, of which 2 were waited for; matrix products, arithmetic and copies ran while one was open for 1% of the time, Pallas kernels for 0%

profile of v1, /device:TPU:8, one launch (start us, length us, event | category | flops | bytes accessed | tf_op | source)
XLA Modules:
  0.0 388.1 jit_solution(12408199539615198185)
XLA Ops:
  0.0 1.9 collective-permute-start.1
  1.9 2.4 collective-permute-start
  4.3 0.8 slice_bitcast_fusion.12
  5.2 20.6 %collective-permute-done.1 = bf16[1,256,4096]{2,1,0:T(8,128)(2,1)S(1)} collective-permute-done((bf16[1,256,4096]{2,1,0:T(8,128)(2,1)}, bf16[1,256,4096]{2,1,0:T(8,128)(2,1)S(1)}, u32[]{:S(2)}, u32[]{:S(2)}) %collective-permute-start.1) | collective-permute-done | bytes 2097184 | tf_op jit(solution)/shard_map/ppermute | solution.py:14
  25.8 0.0 copy-start.1
  25.8 1.3 copy-done.1
  27.1 6.6 %collective-permute-done = bf16[1,256,4096]{2,1,0:T(8,128)(2,1)S(1)} collective-permute-done((bf16[1,256,4096]{2,1,0:T(8,128)(2,1)}, bf16[1,256,4096]{2,1,0:T(8,128)(2,1)S(1)}, u32[]{:S(2)}, u32[]{:S(2)}) %collective-permute-start) | collective-permute-done | bytes 2097184 | tf_op jit(solution)/shard_map/ppermute | solution.py:14
  33.6 0.0 copy-start.3
  33.7 1.3 copy-done.3
  35.0 3.4 stack.27
  38.4 0.0 copy-start.5
  38.4 12.5 %all-to-all-start = ((bf16[32,3,1,8,4096]{4,3,2,1,0:T(8,128)(2,1)}), bf16[32,3,1,8,4096]{4,3,2,1,0:T(8,128)(2,1)}, u32[]{:S(2)}, u32[]{:S(2)}) async-start(bf16[32,3,1,8,4096]{4,3,2,1,0:T(8,128)(2,1)} %stack.27), calls=%async_computation | async-start | bytes 12582912 | tf_op jit(solution)/shard_map/all_to_all | solution.py:48
  50.9 1.9 collective-permute-start.2
  52.9 3.6 collective-permute-start.3
  57.2 0.0 copy-done.5
  57.2 1.3 dynamic-slice
  59.3 0.2 dynamic-update-slice
  59.5 316.4 %all-reduce = bf16[256]{0:T(256)(128)(2,1)S(1)} all-reduce(bf16[256]{0:T(256)(128)(2,1)S(1)} %dynamic-update-slice), channel_id=1, replica_groups=mesh['occ'=16,'vir'=32] {'vir'}, use_global_device_ids=true, to_apply=%add | all-reduce | flops 256 | bytes 1024
  375.9 0.1 add_subtract_fusion
  376.0 0.0 collective-permute-done.2
  376.0 0.0 collective-permute-done.3
  376.0 1.4 maximum_convert_fusion
  377.4 0.0 copy-start
  377.4 0.0 all-to-all-done
  377.4 3.4 copy.10
  380.8 0.0 copy-start.2
  380.8 0.0 copy-start.4
  380.8 0.0 copy-done
  380.8 1.8 fusion.9
  382.7 0.0 copy-done.2
  382.7 0.4 copy-done.4
  383.0 1.8 fusion.14
  384.9 3.2 fusion.5
  (6 shorter events, 0.0 us)
Async XLA Ops:
  0.0 25.8 %collective-permute-start.1 = (bf16[1,256,4096]{2,1,0:T(8,128)(2,1)}, bf16[1,256,4096]{2,1,0:T(8,128)(2,1)S(1)}, u32[]{:S(2)}, u32[]{:S(2)}) collective-permute-start(bf16[1,256,4096]{2,1,0:T(8,128)(2,1)} %param.3), channel_id=1, source_target_pairs={{32,0},{64,32},{96,64},{128,96},{160,128},{192,160},{224,192},{256... | collective-permute-start | bytes 6291464 | tf_op jit(solution)/shard_map/ppermute | solution.py:14
  1.9 31.7 %collective-permute-start = (bf16[1,256,4096]{2,1,0:T(8,128)(2,1)}, bf16[1,256,4096]{2,1,0:T(8,128)(2,1)S(1)}, u32[]{:S(2)}, u32[]{:S(2)}) collective-permute-start(bf16[1,256,4096]{2,1,0:T(8,128)(2,1)} %param.3), channel_id=1, source_target_pairs={{480,0},{0,32},{32,64},{64,96},{96,128},{128,160},{160,192},{192,2... | collective-permute-start | bytes 6291464 | tf_op jit(solution)/shard_map/ppermute | solution.py:14
  25.8 1.3 copy-start.1
  33.6 1.3 copy-start.3
  38.4 18.8 %copy-start.5 = (bf16[256]{0:T(256)(128)(2,1)S(1)}, bf16[256]{0:T(256)(128)(2,1)}, u32[]{:S(2)}) copy-start(bf16[256]{0:T(256)(128)(2,1)} %param.5) | copy-start | bytes 1540
  38.4 339.0 %all-to-all-start = ((bf16[32,3,1,8,4096]{4,3,2,1,0:T(8,128)(2,1)}), bf16[32,3,1,8,4096]{4,3,2,1,0:T(8,128)(2,1)}, u32[]{:S(2)}, u32[]{:S(2)}) async-start(bf16[32,3,1,8,4096]{4,3,2,1,0:T(8,128)(2,1)} %stack.27), calls=%async_computation | async-start | bytes 12582912 | tf_op jit(solution)/shard_map/all_to_all | solution.py:48
  50.9 325.1 %collective-permute-start.2 = (bf16[1]{0:T(256)(128)(2,1)}, bf16[1]{0:T(256)(128)(2,1)}, u32[]{:S(2)}, u32[]{:S(2)}) collective-permute-start(bf16[1]{0:T(256)(128)(2,1)} %param.4), channel_id=1, source_target_pairs={{480,0},{0,32},{32,64},{64,96},{96,128},{128,160},{160,192},{192,2... | collective-permute-start | bytes 14 | tf_op jit(solution)/shard_map/ppermute | solution.py:14
  52.9 323.2 %collective-permute-start.3 = (bf16[1]{0:T(256)(128)(2,1)}, bf16[1]{0:T(256)(128)(2,1)}, u32[]{:S(2)}, u32[]{:S(2)}) collective-permute-start(bf16[1]{0:T(256)(128)(2,1)} %param.4), channel_id=1, source_target_pairs={{32,0},{64,32},{96,64},{128,96},{160,128},{192,160},{224,192},{256... | collective-permute-start | bytes 14 | tf_op jit(solution)/shard_map/ppermute | solution.py:14
  377.4 3.4 copy-start
  380.8 1.9 copy-start.2
  380.8 2.2 copy-start.4
